TPU v7x, 32 devices: a whole 2x2x4 slice. The times are simulated.
32 devices in a mesh: dp: 8 (over y, x, core), ffn: 4 (over z).
Axes of the slice: x: 2, y: 2, z: 4, core: 2. Of those that a mesh axis runs over, the one named last changes fastest.
Arguments:
- seg_input: bfloat16 [2, 8, 512, 1024], P(None, 'dp', 'ffn'), may hold values from -6 to 6
- memory: bfloat16 [2, 8, 384, 1024], P(None, 'dp', 'ffn'), may hold values from -6 to 6
- compressed: bfloat16 [2, 8, 512, 1024], P(None, 'dp', 'ffn'), may hold values from -6 to 6
- mem_fill: int32 [2, 8], P(None, 'dp'), may hold values from 0 to 384, as said below
- comp_fill: int32 [2, 8], P(None, 'dp'), may hold values from 0 to 512, as said below
- attn_gain: float32 [1024], replicated, may hold values from 0.5 to 1.5
- attn_shift: float32 [1024], replicated, may hold values from -1.75 to 1.75
- attn_weights: bfloat16 [4096, 1024], replicated, may hold values from -1.5 to 1.5
- rel_table: float32 [8, 22], replicated, may hold values from -6 to 6
- ffn_gain: float32 [1024], replicated, may hold values from 0.5 to 1.5
- ffn_shift: float32 [1024], replicated, may hold values from -1.75 to 1.75
- w_up: bfloat16 [1024, 4096], P(None, 'ffn'), may hold values from -0.1875 to 0.1875
- b_up: float32 [4096], P('ffn'), may hold values from -1.75 to 1.75
- w_down: bfloat16 [4096, 1024], P('ffn'), may hold values from -0.125 to 0.125
- b_down: float32 [1024], replicated, may hold values from -1.75 to 1.75
- conv_weight: bfloat16 [3072, 1024], replicated, may hold values from -0.109375 to 0.109375
- conv_bias: float32 [1024], replicated, may hold values from -1.75 to 1.75
- out_grad: bfloat16 [2, 8, 512, 1024], P(None, 'dp', 'ffn'), may hold values from -6 to 6
- comp_grad: bfloat16 [2, 8, 128, 1024], P(None, 'dp', 'ffn'), may hold values from -6 to 6
Outputs:
- layer_out: bfloat16 [2, 8, 512, 1024], P(None, 'dp', 'ffn')
- new_compressed: bfloat16 [2, 8, 128, 1024], P(None, 'dp', 'ffn')
- seg_grad: float32 [2, 8, 512, 1024], P(None, 'dp', 'ffn')
- attn_gain_grad: float32 [1024], replicated
- attn_shift_grad: float32 [1024], replicated
- attn_weights_grad: float32 [4096, 1024], P(('dp', 'ffn'))
- rel_table_grad: float32 [8, 22], replicated
- ffn_gain_grad: float32 [1024], replicated
- ffn_shift_grad: float32 [1024], replicated
- w_up_grad: float32 [1024, 4096], P('dp', 'ffn')
- b_up_grad: float32 [4096], replicated
- w_down_grad: float32 [4096, 1024], P('ffn', 'dp')
- b_down_grad: float32 [1024], replicated
- conv_weight_grad: float32 [3072, 1024], replicated
- conv_bias_grad: float32 [1024], replicated
Inputs may be any that keep to these rules, and one draw needn't show every extreme that they name: `mem_fill`: in every micro-batch one stream has all 384 memory slots live and another none; live slots are the newest, at the end of the buffer. `comp_fill`: in every micro-batch one stream has all 512 compressed slots live and another none; live slots are the newest, at the end of the buffer.
All inputs are finite; a program needn't handle non-finite values.
Results may differ from a plain program's by a relative error of at most 0.028.
Values may be sent and summed in bfloat16 or wider, within the bound.
No kernel may reach another device: no remote copies, remote signals or barrier semaphores. Data moves between devices by JAX's collectives and lax.ppermute only.
A program may use at most 320 MiB of HBM per device.

v0:
```python
import jax
import jax.numpy as jnp
from jax import lax
from jax.sharding import PartitionSpec as P

D = 1024
H = 8
HD = 128
M = 384
CM = 512
PW = 64
KR = 1408
NB = 22
EPSILON = 1e-05
MASKED_SCORE = -1e30


def normalize(rows_in, gain, shift):
    centre = jnp.mean(rows_in, axis=-1, keepdims=True)
    centred = rows_in - centre
    variance = jnp.mean(centred * centred, axis=-1, keepdims=True)
    return centred * lax.rsqrt(variance + EPSILON) * gain + shift


def smooth_unit(values_in):
    return jax.nn.gelu(values_in, approximate=False)


def matmul(left, right):
    return jnp.dot(left, right, preferred_element_type=jnp.float32)


def contract_rows(left, right):
    return lax.dot_general(
        left, right, (((0,), (0,)), ((), ())), preferred_element_type=jnp.float32
    )


def times_transposed(left, right):
    return lax.dot_general(
        left, right, (((1,), (1,)), ((), ())), preferred_element_type=jnp.float32
    )


def norm_backward(rows_in, gain, shift, cotangent):
    outputs, pullback = jax.vjp(normalize, rows_in, gain, shift)
    return pullback(cotangent)


def on_device(
    seg_input,
    memory,
    compressed,
    mem_fill,
    comp_fill,
    attn_gain,
    attn_shift,
    attn_weights,
    rel_table,
    ffn_gain,
    ffn_shift,
    w_up,
    b_up,
    w_down,
    b_down,
    conv_weight,
    conv_bias,
    out_grad,
    comp_grad,
):
    groups = lax.axis_size("ffn")
    ffn_rank = lax.axis_index("ffn")
    seg_rows = seg_input.shape[2]
    mem_rows = memory.shape[2]
    hidden_local = w_up.shape[1]
    query_tiles = seg_rows // PW
    score_scale = HD ** (-0.5)
    w_query = attn_weights[:D]
    w_key = attn_weights[D : 2 * D]
    w_value = attn_weights[2 * D : 3 * D]
    w_out = attn_weights[3 * D :]
    key_pos = jnp.arange(KR, dtype=jnp.int32)
    query_pos = CM + M + ffn_rank * seg_rows + jnp.arange(seg_rows, dtype=jnp.int32)
    query_blocks = (
        (CM + M) // PW + ffn_rank * query_tiles + jnp.arange(query_tiles, dtype=jnp.int32)
    )
    distance = query_blocks[:, None] - jnp.arange(NB, dtype=jnp.int32)[None, :]
    one_hot = (distance[:, :, None] == jnp.arange(NB, dtype=jnp.int32)[None, None, :]).astype(
        jnp.float32
    )
    tile_bias = jnp.einsum("hn,qkn->hqk", rel_table, one_hot, precision=lax.Precision.HIGHEST)
    memory_pos = ffn_rank * mem_rows + jnp.arange(mem_rows, dtype=jnp.int32)

    def scores_of(queries, key_heads, key_mask):
        raw_scores = (
            jnp.einsum("qhd,khd->hqk", queries, key_heads, preferred_element_type=jnp.float32)
            * score_scale
        )
        tiled = raw_scores.reshape(H, query_tiles, PW, NB, PW) + tile_bias[:, :, None, :, None]
        return jnp.where(key_mask[None], tiled.reshape(H, seg_rows, KR), MASKED_SCORE)

    def micro_batch(totals, sample):
        segment, memory_now, compressed_now, mem_count, comp_count, grad_rows_in, comp_cot = sample
        segment_f = segment.astype(jnp.float32)
        sources = (compressed_now.astype(jnp.float32), memory_now.astype(jnp.float32), segment_f)
        lowered = [
            normalize(section, attn_gain, attn_shift).astype(jnp.bfloat16) for section in sources
        ]
        own_keys = [matmul(section, w_key).astype(jnp.bfloat16) for section in lowered]
        own_values = [matmul(section, w_value).astype(jnp.bfloat16) for section in lowered]
        gathered = (
            lax.all_gather(own_keys[0], "ffn", axis=0, tiled=True),
            lax.all_gather(own_keys[1], "ffn", axis=0, tiled=True),
            lax.all_gather(own_keys[2], "ffn", axis=0, tiled=True),
            lax.all_gather(own_values[0], "ffn", axis=0, tiled=True),
            lax.all_gather(own_values[1], "ffn", axis=0, tiled=True),
            lax.all_gather(own_values[2], "ffn", axis=0, tiled=True),
        )
        key_heads = jnp.concatenate(gathered[:3], axis=0).reshape(KR, H, HD)
        value_heads = jnp.concatenate(gathered[3:], axis=0).reshape(KR, H, HD)
        queries = matmul(lowered[2], w_query).astype(jnp.bfloat16).reshape(seg_rows, H, HD)
        live_keys = jnp.where(
            key_pos < CM,
            key_pos >= CM - comp_count,
            jnp.where(key_pos < CM + M, key_pos >= CM + M - mem_count, True),
        )
        key_mask = live_keys[None, :] & (key_pos[None, :] <= query_pos[:, None])
        scores = scores_of(queries, key_heads, key_mask)
        row_max = jnp.max(scores, axis=-1, keepdims=True)
        expanded = jnp.exp(scores - row_max)
        row_total = jnp.sum(expanded, axis=-1, keepdims=True)
        log_total = row_max + jnp.log(row_total)
        attention = (expanded / row_total).astype(jnp.bfloat16)
        mixed_heads = jnp.einsum(
            "hqk,khd->qhd", attention, value_heads, preferred_element_type=jnp.float32
        )
        mixed_heads = mixed_heads.reshape(seg_rows, D).astype(jnp.bfloat16)
        residual = segment_f + matmul(mixed_heads, w_out)
        ffn_in = normalize(residual, ffn_gain, ffn_shift).astype(jnp.bfloat16)
        ffn_rows = lax.all_gather(ffn_in, "ffn", axis=0, tiled=True)
        hidden_pre = matmul(ffn_rows, w_up) + b_up
        activated_f, smooth_pull = jax.vjp(smooth_unit, hidden_pre)
        activated = activated_f.astype(jnp.bfloat16)
        branch = lax.psum_scatter(
            matmul(activated, w_down).astype(jnp.bfloat16), "ffn", scatter_dimension=0, tiled=True
        ).astype(jnp.float32)
        layer_rows = (residual + branch + b_down).astype(jnp.bfloat16)
        alive_rows = memory_pos >= M - mem_count
        flat_memory = jnp.where(
            alive_rows[:, None], memory_now, jnp.zeros_like(memory_now)
        ).reshape(mem_rows // 3, 3 * D)
        compressed_new = (matmul(flat_memory, conv_weight) + conv_bias).astype(jnp.bfloat16)
        grad_out = grad_rows_in.astype(jnp.float32)
        grad_all = lax.all_gather(grad_rows_in, "ffn", axis=0, tiled=True)
        grad_hidden = times_transposed(grad_all, w_down)
        grad_pre = smooth_pull(grad_hidden)[0].astype(jnp.bfloat16)
        down_grad = contract_rows(activated, grad_all)
        up_grad = contract_rows(ffn_rows, grad_pre)
        up_bias_part = jnp.sum(grad_pre.astype(jnp.float32), axis=0)
        grad_ffn_in = lax.psum_scatter(
            times_transposed(grad_pre, w_up).astype(jnp.bfloat16),
            "ffn",
            scatter_dimension=0,
            tiled=True,
        ).astype(jnp.float32)
        grad_normal, ffn_gain_part, ffn_shift_part = norm_backward(
            residual, ffn_gain, ffn_shift, grad_ffn_in
        )
        grad_residual = grad_out + grad_normal
        grad_branch = grad_residual.astype(jnp.bfloat16)
        out_weight_grad = contract_rows(mixed_heads, grad_branch)
        grad_mixed = (
            times_transposed(grad_branch, w_out).astype(jnp.bfloat16).reshape(seg_rows, H, HD)
        )
        scores_again = scores_of(queries, key_heads, key_mask)
        attention_f = jnp.exp(scores_again - log_total)
        grad_attention = jnp.einsum(
            "qhd,khd->hqk", grad_mixed, value_heads, preferred_element_type=jnp.float32
        )
        row_inner = jnp.sum(attention_f * grad_attention, axis=-1, keepdims=True)
        grad_scores = (attention_f * (grad_attention - row_inner)).astype(jnp.bfloat16)
        tile_grad = jnp.sum(
            grad_scores.astype(jnp.float32).reshape(H, query_tiles, PW, NB, PW), axis=(2, 4)
        )
        table_grad = jnp.einsum("hqk,qkn->hn", tile_grad, one_hot, precision=lax.Precision.HIGHEST)
        grad_query = (
            jnp.einsum("hqk,khd->qhd", grad_scores, key_heads, preferred_element_type=jnp.float32)
            * score_scale
        )
        grad_query = grad_query.reshape(seg_rows, D).astype(jnp.bfloat16)
        key_part = (
            jnp.einsum(
                "hqk,qhd->khd", grad_scores, queries, preferred_element_type=jnp.float32
            ).reshape(KR, D)
            * score_scale
        )
        value_part = jnp.einsum(
            "hqk,qhd->khd",
            attention_f.astype(jnp.bfloat16),
            grad_mixed,
            preferred_element_type=jnp.float32,
        ).reshape(KR, D)
        own_grads = (
            lax.psum_scatter(
                key_part[:CM].astype(jnp.bfloat16), "ffn", scatter_dimension=0, tiled=True
            ).astype(jnp.float32),
            lax.psum_scatter(
                key_part[CM : CM + M].astype(jnp.bfloat16), "ffn", scatter_dimension=0, tiled=True
            ).astype(jnp.float32),
            lax.psum_scatter(
                key_part[CM + M :].astype(jnp.bfloat16), "ffn", scatter_dimension=0, tiled=True
            ).astype(jnp.float32),
            lax.psum_scatter(
                value_part[:CM].astype(jnp.bfloat16), "ffn", scatter_dimension=0, tiled=True
            ).astype(jnp.float32),
            lax.psum_scatter(
                value_part[CM : CM + M].astype(jnp.bfloat16), "ffn", scatter_dimension=0, tiled=True
            ).astype(jnp.float32),
            lax.psum_scatter(
                value_part[CM + M :].astype(jnp.bfloat16), "ffn", scatter_dimension=0, tiled=True
            ).astype(jnp.float32),
        )
        grad_keys = [section.astype(jnp.bfloat16) for section in own_grads[:3]]
        grad_values = [section.astype(jnp.bfloat16) for section in own_grads[3:]]
        grad_normed = [
            times_transposed(grad_keys[section_id], w_key)
            + times_transposed(grad_values[section_id], w_value)
            for section_id in range(3)
        ]
        grad_normed[2] = grad_normed[2] + times_transposed(grad_query, w_query)
        query_weight_grad = contract_rows(lowered[2], grad_query)
        key_weight_grad = (
            contract_rows(lowered[0], grad_keys[0])
            + contract_rows(lowered[1], grad_keys[1])
            + contract_rows(lowered[2], grad_keys[2])
        )
        value_weight_grad = (
            contract_rows(lowered[0], grad_values[0])
            + contract_rows(lowered[1], grad_values[1])
            + contract_rows(lowered[2], grad_values[2])
        )
        norm_parts = [
            norm_backward(sources[section_id], attn_gain, attn_shift, grad_normed[section_id])
            for section_id in range(3)
        ]
        grad_segment = grad_residual + norm_parts[2][0]
        attn_gain_part = norm_parts[0][1] + norm_parts[1][1] + norm_parts[2][1]
        attn_shift_part = norm_parts[0][2] + norm_parts[1][2] + norm_parts[2][2]
        conv_grad = contract_rows(flat_memory, comp_cot)
        conv_bias_part = jnp.sum(comp_cot.astype(jnp.float32), axis=0)
        down_bias_part = jnp.sum(grad_out, axis=0)
        updates = (
            attn_gain_part,
            attn_shift_part,
            query_weight_grad,
            key_weight_grad,
            value_weight_grad,
            out_weight_grad,
            table_grad,
            ffn_gain_part,
            ffn_shift_part,
            up_grad,
            up_bias_part,
            down_grad,
            down_bias_part,
            conv_grad,
            conv_bias_part,
        )
        totals = jax.tree.map(jnp.add, totals, updates)
        return (totals, (layer_rows, compressed_new, grad_segment))

    float_zero = jnp.float32
    zero_grads = (
        jnp.zeros((D,), float_zero),
        jnp.zeros((D,), float_zero),
        jnp.zeros((D, D), float_zero),
        jnp.zeros((D, D), float_zero),
        jnp.zeros((D, D), float_zero),
        jnp.zeros((D, D), float_zero),
        jnp.zeros(rel_table.shape, float_zero),
        jnp.zeros((D,), float_zero),
        jnp.zeros((D,), float_zero),
        jnp.zeros(w_up.shape, float_zero),
        jnp.zeros((hidden_local,), float_zero),
        jnp.zeros(w_down.shape, float_zero),
        jnp.zeros((D,), float_zero),
        jnp.zeros(conv_weight.shape, float_zero),
        jnp.zeros((D,), float_zero),
    )
    samples = (
        seg_input[:, 0],
        memory[:, 0],
        compressed[:, 0],
        mem_fill[:, 0],
        comp_fill[:, 0],
        out_grad[:, 0],
        comp_grad[:, 0],
    )
    totals, stacked = lax.scan(micro_batch, zero_grads, samples)
    attn_grad = jnp.concatenate([totals[2], totals[3], totals[4], totals[5]], axis=0)
    attn_grad = lax.psum_scatter(attn_grad, ("dp", "ffn"), scatter_dimension=0, tiled=True)
    up_weight_grad, down_weight_grad = (
        lax.psum_scatter(totals[9], "dp", scatter_dimension=0, tiled=True),
        lax.psum_scatter(totals[11], "dp", scatter_dimension=1, tiled=True),
    )
    up_bias_full = lax.dynamic_update_slice(
        jnp.zeros((hidden_local * groups,), jnp.float32), totals[10], (ffn_rank * hidden_local,)
    )
    shared = lax.psum(
        (
            totals[13],
            totals[14],
            totals[0],
            totals[1],
            totals[7],
            totals[8],
            totals[12],
            totals[6],
            up_bias_full,
        ),
        ("dp", "ffn"),
    )
    return (
        stacked[0][:, None],
        stacked[1][:, None],
        stacked[2][:, None],
        shared[2],
        shared[3],
        attn_grad,
        shared[7],
        shared[4],
        shared[5],
        up_weight_grad,
        shared[8],
        down_weight_grad,
        shared[6],
        shared[0],
        shared[1],
    )


def solution(mesh):
    return jax.shard_map(
        on_device,
        mesh=mesh,
        in_specs=(
            P(None, "dp", "ffn", None),
            P(None, "dp", "ffn", None),
            P(None, "dp", "ffn", None),
            P(None, "dp"),
            P(None, "dp"),
            P(),
            P(),
            P(),
            P(),
            P(),
            P(),
            P(None, "ffn"),
            P("ffn"),
            P("ffn", None),
            P(),
            P(),
            P(),
            P(None, "dp", "ffn", None),
            P(None, "dp", "ffn", None),
        ),
        out_specs=(
            P(None, "dp", "ffn", None),
            P(None, "dp", "ffn", None),
            P(None, "dp", "ffn", None),
            P(),
            P(),
            P(("dp", "ffn"), None),
            P(),
            P(),
            P(),
            P("dp", "ffn"),
            P(),
            P("ffn", "dp"),
            P(),
            P(),
            P(),
        ),
        check_vma=False,
    )
```

profile of v0, /device:TPU:0, one launch (start us, length us, event | category | flops | bytes accessed | tf_op | source)
XLA Modules:
  0.0 1478.6 jit_solution(13740428444911833908)
XLA Ops:
  15.3 883.2 %while.46 = (s32[]{:T(128)}, f32[1024]{0:T(1024)}, f32[1024]{0:T(1024)}, f32[1024,1024]{1,0:T(8,128)}, f32[1024,1024]{1,0:T(8,128)}, /*index=5*/f32[1024,1024]{1...) while((s32[]{:T(128)}, f32[1024]{0:T(1024)}, ...), condition=%wide.region_36.37_spmd.clone.clone, body=%wide.region_0.36_spmd.clone.clone.sunk | while | flops 15250011136 | bytes 700114752 | solution.py:299
  27.5 31.8 %all_gather.47 = bf16[384,1024]{1,0:T(8,128)(2,1)} all-gather(bf16[96,1024]{1,0:T(8,128)(2,1)S(1)} %convolution_convert_fusion.23), channel_id=1, replica_groups=mesh['dp'=8,'ffn'=4] {'ffn'}, dimensions={0}, use_global_device_ids=true | all-gather | bytes 983040 | tf_op jit(solution)/shard_map/while/body/eval_jaxpr/all_gather | solution.py:113
  67.8 11.7 add.700
  87.2 21.5 %all_gather.50 = bf16[384,1024]{1,0:T(8,128)(2,1)} all-gather(bf16[96,1024]{1,0:T(8,128)(2,1)S(1)} %convolution_convert_fusion.26), channel_id=1, replica_groups=mesh['dp'=8,'ffn'=4] {'ffn'}, dimensions={0}, use_global_device_ids=true | all-gather | bytes 983040 | tf_op jit(solution)/shard_map/while/body/eval_jaxpr/all_gather | solution.py:116
  125.5 26.4 %all-gather.17.cloned.1.call-done = bf16[512,1024]{1,0:T(8,128)(2,1)} async-done(((bf16[128,1024]{1,0:T(8,128)(2,1)}), bf16[512,1024]{1,0:T(8,128)(2,1)}) %all-gather.17.cloned.1.call-update) | async-done | bytes 1048592 | tf_op jit(solution)/shard_map/while/body/eval_jaxpr/all_gather | solution.py:115
  162.1 24.7 %all-gather.19.cloned.1.call-done = bf16[512,1024]{1,0:T(8,128)(2,1)} async-done(((bf16[128,1024]{1,0:T(8,128)(2,1)}), bf16[512,1024]{1,0:T(8,128)(2,1)}) %all-gather.19.cloned.1.call-update) | async-done | bytes 1048592 | tf_op jit(solution)/shard_map/while/body/eval_jaxpr/all_gather | solution.py:140
  186.7 8.7 multiply_convert_fusion.5
  195.4 20.8 %all-gather.21.cloned.1.call-done = bf16[1,512,1024]{2,1,0:T(8,128)(2,1)} async-done(((bf16[1,128,1024]{2,1,0:T(8,128)(2,1)}), bf16[1,512,1024]{2,1,0:T(8,128)(2,1)}) %all-gather.21.cloned.1.call-update) | async-done | bytes 1048592 | tf_op jit(solution)/shard_map/while/body/eval_jaxpr/all_gather | solution.py:154
  229.6 22.5 %reduce-scatter.42.cloned.1.call-done = bf16[128,1024]{1,0:T(8,128)(2,1)} async-done(((bf16[512,1024]{1,0:T(8,128)(2,1)}), bf16[128,1024]{1,0:T(8,128)(2,1)}) %reduce-scatter.42.cloned.1.call-update) | async-done | bytes 262160 | tf_op jit(solution)/shard_map/while/body/eval_jaxpr/reduce_scatter | solution.py:160
  328.8 11.9 reshape.355
  340.7 10.8 reduce_sum.432
  376.1 10.1 reduce-scatter.46.cloned.1.call-done
  392.4 21.9 %reduce-scatter.48.cloned.1.call-done = bf16[128,1024]{1,0:T(8,128)(2,1)} async-done(((bf16[512,1024]{1,0:T(8,128)(2,1)}), bf16[128,1024]{1,0:T(8,128)(2,1)}) %reduce-scatter.48.cloned.1.call-update) | async-done | bytes 262160 | tf_op jit(solution)/shard_map/while
  416.9 25.5 %reduce-scatter.50.cloned.1.call-done = bf16[128,1024]{1,0:T(8,128)(2,1)} async-done(((bf16[512,1024]{1,0:T(8,128)(2,1)}), bf16[128,1024]{1,0:T(8,128)(2,1)}) %reduce-scatter.50.cloned.1.call-update) | async-done | bytes 262160 | tf_op jit(solution)/shard_map/while
  469.7 30.1 %all_gather.47 = bf16[384,1024]{1,0:T(8,128)(2,1)} all-gather(bf16[96,1024]{1,0:T(8,128)(2,1)S(1)} %convolution_convert_fusion.23), channel_id=1, replica_groups=mesh['dp'=8,'ffn'=4] {'ffn'}, dimensions={0}, use_global_device_ids=true | all-gather | bytes 983040 | tf_op jit(solution)/shard_map/while/body/eval_jaxpr/all_gather | solution.py:113
  508.4 11.7 add.700
  527.8 20.5 %all_gather.50 = bf16[384,1024]{1,0:T(8,128)(2,1)} all-gather(bf16[96,1024]{1,0:T(8,128)(2,1)S(1)} %convolution_convert_fusion.26), channel_id=1, replica_groups=mesh['dp'=8,'ffn'=4] {'ffn'}, dimensions={0}, use_global_device_ids=true | all-gather | bytes 983040 | tf_op jit(solution)/shard_map/while/body/eval_jaxpr/all_gather | solution.py:116
  565.1 24.6 %all-gather.17.cloned.1.call-done = bf16[512,1024]{1,0:T(8,128)(2,1)} async-done(((bf16[128,1024]{1,0:T(8,128)(2,1)}), bf16[512,1024]{1,0:T(8,128)(2,1)}) %all-gather.17.cloned.1.call-update) | async-done | bytes 1048592 | tf_op jit(solution)/shard_map/while/body/eval_jaxpr/all_gather | solution.py:115
  599.6 25.0 %all-gather.19.cloned.1.call-done = bf16[512,1024]{1,0:T(8,128)(2,1)} async-done(((bf16[128,1024]{1,0:T(8,128)(2,1)}), bf16[512,1024]{1,0:T(8,128)(2,1)}) %all-gather.19.cloned.1.call-update) | async-done | bytes 1048592 | tf_op jit(solution)/shard_map/while/body/eval_jaxpr/all_gather | solution.py:140
  624.6 8.7 multiply_convert_fusion.5
  633.3 20.8 %all-gather.21.cloned.1.call-done = bf16[1,512,1024]{2,1,0:T(8,128)(2,1)} async-done(((bf16[1,128,1024]{2,1,0:T(8,128)(2,1)}), bf16[1,512,1024]{2,1,0:T(8,128)(2,1)}) %all-gather.21.cloned.1.call-update) | async-done | bytes 1048592 | tf_op jit(solution)/shard_map/while/body/eval_jaxpr/all_gather | solution.py:154
  667.5 22.5 %reduce-scatter.42.cloned.1.call-done = bf16[128,1024]{1,0:T(8,128)(2,1)} async-done(((bf16[512,1024]{1,0:T(8,128)(2,1)}), bf16[128,1024]{1,0:T(8,128)(2,1)}) %reduce-scatter.42.cloned.1.call-update) | async-done | bytes 262160 | tf_op jit(solution)/shard_map/while/body/eval_jaxpr/reduce_scatter | solution.py:160
  741.8 11.2 select_add_fusion.35
  774.8 11.9 reshape.355
  786.7 11.0 reduce_sum.432
  832.1 20.0 %reduce-scatter.48.cloned.1.call-done = bf16[128,1024]{1,0:T(8,128)(2,1)} async-done(((bf16[512,1024]{1,0:T(8,128)(2,1)}), bf16[128,1024]{1,0:T(8,128)(2,1)}) %reduce-scatter.48.cloned.1.call-update) | async-done | bytes 262160 | tf_op jit(solution)/shard_map/while
  854.7 25.6 %reduce-scatter.50.cloned.1.call-done = bf16[128,1024]{1,0:T(8,128)(2,1)} async-done(((bf16[512,1024]{1,0:T(8,128)(2,1)}), bf16[128,1024]{1,0:T(8,128)(2,1)}) %reduce-scatter.50.cloned.1.call-update) | async-done | bytes 262160 | tf_op jit(solution)/shard_map/while
  900.5 12.7 pad_maximum_fusion.1
  914.1 40.6 %all-reduce = (f32[1024]{0:T(1024)}, f32[1024]{0:T(1024)}, f32[8,22]{1,0:T(8,128)}, f32[1024]{0:T(1024)}, f32[1024]{0:T(1024)}, /*index=5*/f32[4096]{0:T(1024)}, f32[1024]{0:T(1024)}, f32[1024]{0:T(1024)}) all-reduce(f32[1024]{0:T(1024)S(1)} %copy-done.75, f32[1024]{0:T(1024)S(1)} %copy-done.78, ...), channel_id=1, replica_groups=mesh['dp'=8,'ffn'=4] {'dp','ffn'}, use_global_device_ids=true, to_apply=%region_37.38 | all-reduce | flops 10416 | bytes 83328 | tf_op jit(solution)/shard_map/psum | solution.py:309
  954.8 400.1 %all-reduce.3.cloned.1.call-done = f32[3072,1024]{1,0:T(8,128)} async-done(((f32[3072,1024]{1,0:T(8,128)}), f32[3072,1024]{1,0:T(8,128)}) %all-reduce.3.cloned.1.call-update) | async-done | bytes 12582928 | tf_op jit(solution)/shard_map/psum | solution.py:309
  1354.8 104.0 %reduce-scatter.36.cloned.1.call-done = f32[128,1024]{1,0:T(8,128)} async-done(((f32[4096,1024]{1,0:T(8,128)}), f32[128,1024]{1,0:T(8,128)}) %reduce-scatter.36.cloned.1.call-update) | async-done | bytes 524304 | tf_op jit(solution)/shard_map/reduce_scatter | solution.py:301
  1458.8 12.1 copy.190
  (685 shorter events, 391.0 us)
Async XLA Ops:
  15.6 93.1 %all-gather.11.cloned.1.call-start = ((), (), s32[]{:S(2)}) async-start(), calls=%async_computation.15 | async-start | bytes 1310720 | tf_op jit(solution)/shard_map/while/body/eval_jaxpr/all_gather | solution.py:114
  17.3 91.4 %all-gather.13.cloned.1.call-start = ((), (), s32[]{:S(2)}) async-start(), calls=%async_computation.16 | async-start | bytes 1310720 | tf_op jit(solution)/shard_map/while/body/eval_jaxpr/all_gather | solution.py:112
  19.0 106.5 %all-gather.15.cloned.1.call-start = ((), (), s32[]{:S(2)}) async-start(), calls=%async_computation.17 | async-start | bytes 1310720 | tf_op jit(solution)/shard_map/while/body/eval_jaxpr/all_gather | solution.py:117
  22.0 129.9 %all-gather.17.cloned.1.call-start = ((), (), s32[]{:S(2)}) async-start(), calls=%async_computation.18 | async-start | bytes 1310720 | tf_op jit(solution)/shard_map/while/body/eval_jaxpr/all_gather | solution.py:115
  24.9 161.8 %all-gather.19.cloned.1.call-start = ((), (), s32[]{:S(2)}) async-start(), calls=%async_computation.19 | async-start | bytes 1310720 | tf_op jit(solution)/shard_map/while/body/eval_jaxpr/all_gather | solution.py:140
  159.1 57.0 %all-gather.21.cloned.1.call-start = ((), (), s32[]{:S(2)}) async-start(), calls=%async_computation.20 | async-start | bytes 1310720 | tf_op jit(solution)/shard_map/while/body/eval_jaxpr/all_gather | solution.py:154
  161.5 90.6 %reduce-scatter.42.cloned.1.call-start = ((), (), s32[]{:S(2)}) async-start(), calls=%async_computation.21 | async-start | bytes 1310720 | tf_op jit(solution)/shard_map/while/body/eval_jaxpr/reduce_scatter | solution.py:160
  225.3 137.8 %reduce-scatter.56.cloned.1.call-start = ((), (), s32[]{:S(2)}) async-start(), calls=%async_computation.28 | async-start | bytes 1310720 | tf_op jit(solution)/shard_map/while/body/eval_jaxpr/reduce_scatter | solution.py:144
  229.6 135.3 %reduce-scatter.52.cloned.1.call-start = ((), (), s32[]{:S(2)}) async-start(), calls=%async_computation.26 | async-start | bytes 983040 | tf_op jit(solution)/shard_map/while
  274.1 95.4 %reduce-scatter.54.cloned.1.call-start = ((), (), s32[]{:S(2)}) async-start(), calls=%async_computation.27 | async-start | bytes 983040 | tf_op jit(solution)/shard_map/while
  283.1 91.2 %reduce-scatter.44.cloned.1.call-start = ((), (), s32[]{:S(2)}) async-start(), calls=%async_computation.22 | async-start | bytes 1310720 | tf_op jit(solution)/shard_map/while
  288.5 97.7 %reduce-scatter.46.cloned.1.call-start = ((), (), s32[]{:S(2)}) async-start(), calls=%async_computation.23 | async-start | bytes 1310720 | tf_op jit(solution)/shard_map/while
  294.0 120.3 %reduce-scatter.48.cloned.1.call-start = ((), (), s32[]{:S(2)}) async-start(), calls=%async_computation.24 | async-start | bytes 1310720 | tf_op jit(solution)/shard_map/while
  312.8 129.5 %reduce-scatter.50.cloned.1.call-start = ((), (), s32[]{:S(2)}) async-start(), calls=%async_computation.25 | async-start | bytes 1310720 | tf_op jit(solution)/shard_map/while
  457.8 90.5 %all-gather.11.cloned.1.call-start = ((), (), s32[]{:S(2)}) async-start(), calls=%async_computation.15 | async-start | bytes 1310720 | tf_op jit(solution)/shard_map/while/body/eval_jaxpr/all_gather | solution.py:114
  459.5 88.8 %all-gather.13.cloned.1.call-start = ((), (), s32[]{:S(2)}) async-start(), calls=%async_computation.16 | async-start | bytes 1310720 | tf_op jit(solution)/shard_map/while/body/eval_jaxpr/all_gather | solution.py:112
  461.2 103.9 %all-gather.15.cloned.1.call-start = ((), (), s32[]{:S(2)}) async-start(), calls=%async_computation.17 | async-start | bytes 1310720 | tf_op jit(solution)/shard_map/while/body/eval_jaxpr/all_gather | solution.py:117
  464.2 125.6 %all-gather.17.cloned.1.call-start = ((), (), s32[]{:S(2)}) async-start(), calls=%async_computation.18 | async-start | bytes 1310720 | tf_op jit(solution)/shard_map/while/body/eval_jaxpr/all_gather | solution.py:115
  467.1 157.5 %all-gather.19.cloned.1.call-start = ((), (), s32[]{:S(2)}) async-start(), calls=%async_computation.19 | async-start | bytes 1310720 | tf_op jit(solution)/shard_map/while/body/eval_jaxpr/all_gather | solution.py:140
  597.0 57.0 %all-gather.21.cloned.1.call-start = ((), (), s32[]{:S(2)}) async-start(), calls=%async_computation.20 | async-start | bytes 1310720 | tf_op jit(solution)/shard_map/while/body/eval_jaxpr/all_gather | solution.py:154
  599.4 90.6 %reduce-scatter.42.cloned.1.call-start = ((), (), s32[]{:S(2)}) async-start(), calls=%async_computation.21 | async-start | bytes 1310720 | tf_op jit(solution)/shard_map/while/body/eval_jaxpr/reduce_scatter | solution.py:160
  663.2 149.7 %reduce-scatter.56.cloned.1.call-start = ((), (), s32[]{:S(2)}) async-start(), calls=%async_computation.28 | async-start | bytes 1310720 | tf_op jit(solution)/shard_map/while/body/eval_jaxpr/reduce_scatter | solution.py:144
  667.4 147.2 %reduce-scatter.52.cloned.1.call-start = ((), (), s32[]{:S(2)}) async-start(), calls=%async_computation.26 | async-start | bytes 983040 | tf_op jit(solution)/shard_map/while
  712.0 107.3 %reduce-scatter.54.cloned.1.call-start = ((), (), s32[]{:S(2)}) async-start(), calls=%async_computation.27 | async-start | bytes 983040 | tf_op jit(solution)/shard_map/while
  721.0 103.1 %reduce-scatter.44.cloned.1.call-start = ((), (), s32[]{:S(2)}) async-start(), calls=%async_computation.22 | async-start | bytes 1310720 | tf_op jit(solution)/shard_map/while
  726.4 99.5 %reduce-scatter.46.cloned.1.call-start = ((), (), s32[]{:S(2)}) async-start(), calls=%async_computation.23 | async-start | bytes 1310720 | tf_op jit(solution)/shard_map/while
  731.9 120.2 %reduce-scatter.48.cloned.1.call-start = ((), (), s32[]{:S(2)}) async-start(), calls=%async_computation.24 | async-start | bytes 1310720 | tf_op jit(solution)/shard_map/while
  755.4 125.0 %reduce-scatter.50.cloned.1.call-start = ((), (), s32[]{:S(2)}) async-start(), calls=%async_computation.25 | async-start | bytes 1310720 | tf_op jit(solution)/shard_map/while
  898.5 456.3 %all-reduce.3.cloned.1.call-start = ((), (), s32[]{:S(2)}) async-start(), calls=%async_computation.14 | async-start | bytes 25165824 | tf_op jit(solution)/shard_map/psum | solution.py:309
  899.1 455.8 %reduce-scatter.38.cloned.1.call-start = ((), (), s32[]{:S(2)}) async-start(), calls=%async_computation.12 | async-start | bytes 4718592 | tf_op jit(solution)/shard_map/reduce_scatter | solution.py:303
  899.8 455.0 %reduce-scatter.40.cloned.1.call-start = ((), (), s32[]{:S(2)}) async-start(), calls=%async_computation.13 | async-start | bytes 4718592 | tf_op jit(solution)/shard_map/reduce_scatter | solution.py:304
  900.4 558.4 %reduce-scatter.36.cloned.1.call-start = ((), (), s32[]{:S(2)}) async-start(), calls=%async_computation.11 | async-start | bytes 17301504 | tf_op jit(solution)/shard_map/reduce_scatter | solution.py:301
  (185 other events, 1737.2 us)
Sparse Core Ops, SparseCore 0:
  18.6 43.2 all-gather.10
  63.5 27.4 all-gather.12
  92.6 30.4 all-gather.14
  124.4 27.3 all-gather.16
  159.2 27.4 all-gather.18
  188.7 27.4 all-gather.20
  225.4 26.6 reduce-scatter.41
  254.5 25.8 reduce-scatter.55
  282.7 21.9 reduce-scatter.51
  306.8 22.5 reduce-scatter.53
  331.7 26.4 reduce-scatter.43
  360.4 25.7 reduce-scatter.45
  388.5 25.7 reduce-scatter.47
  416.6 25.7 reduce-scatter.49
  460.5 39.7 all-gather.10
  501.7 26.9 all-gather.12
  530.1 30.8 all-gather.14
  562.5 27.2 all-gather.16
  597.1 27.4 all-gather.18
  626.6 27.4 all-gather.20
  663.3 26.6 reduce-scatter.41
  692.4 25.8 reduce-scatter.55
  720.6 21.9 reduce-scatter.51
  744.7 22.5 reduce-scatter.53
  769.6 26.4 reduce-scatter.43
  798.3 25.7 reduce-scatter.45
  826.3 25.7 reduce-scatter.47
  854.5 25.7 reduce-scatter.49
  903.9 51.9 reduce-scatter.37
  960.0 51.9 reduce-scatter.39
  1014.9 443.9 reduce-scatter.35
Sparse Core Ops, SparseCore 1:
  905.6 449.2 all-reduce.2
where the time goes:
time: 1480 us
  waiting for transfers between devices  797 us (54%)
  matrix products  233 us (16%)
  local copies, waits for them, and re-layouts  197 us (13%)
  blocking collectives  145 us (10%)
  other arithmetic  78.2 us (5%)
  between operations  16.1 us (1%)
    psum x1, waiting for transfers between devices, on_device(): lax.psum((totals[13], totals[14], totals[0], totals[1], totals[7], totals...  400 us
    reduce_scatter x1, waiting for transfers between devices, on_device(): lax.psum_scatter(attn_grad, ('dp', 'ffn'), scatter_dimension=0, tiled=True)  104 us
    while x40, waiting for transfers between devices  104 us
    dot_general x22, matrix products, contract_rows(): lax.dot_general(left, right, (((0,), (0,)), ((), ())), preferred_element_...  78.7 us
    all_gather x2, blocking collectives, micro_batch(): lax.all_gather(own_keys[1], 'ffn', axis=0, tiled=True)  61.9 us
    while x348, local copies, waits for them, and re-layouts  60.1 us
    dot_general x22, matrix products, matmul(): return jnp.dot(left, right, preferred_element_type=jnp.float32)  57.1 us
    all_gather x2, waiting for transfers between devices, micro_batch(): lax.all_gather(own_values[0], 'ffn', axis=0, tiled=True)  51 us
  transfers between devices with their start and end apart: 32, of which 15 were waited for; matrix products, arithmetic and copies ran while one was open for 28% of the time, Pallas kernels for 0%

commit v1 on v0

--- a/solution.py
+++ b/solution.py
@@ -151,7 +151,13 @@
         ).reshape(mem_rows // 3, 3 * D)
         compressed_new = (matmul(flat_memory, conv_weight) + conv_bias).astype(jnp.bfloat16)
         grad_out = grad_rows_in.astype(jnp.float32)
-        grad_all = lax.all_gather(grad_rows_in, "ffn", axis=0, tiled=True)
+        size = lax.axis_size("ffn")
+        held, blocks = (grad_rows_in, [grad_rows_in])
+        for _ in range(size - 1):
+            held = lax.ppermute(held, "ffn", [(i, (i + 1) % size) for i in range(size)])
+            blocks.insert(0, held)
+        merged = jnp.concatenate(blocks, axis=0)
+        grad_all = jnp.roll(merged, (lax.axis_index("ffn") + 1) * grad_rows_in.shape[0], axis=0)
         grad_hidden = times_transposed(grad_all, w_down)
         grad_pre = smooth_pull(grad_hidden)[0].astype(jnp.bfloat16)
         down_grad = contract_rows(activated, grad_all)

time: 1480 us -> 1480 us (level)
  waiting for transfers between devices: 797 us -> 749 us
  local copies, waits for them, and re-layouts: 197 us -> 225 us
    all_gather x2, waiting for transfers between devices: 49.7 us -> 0.01 us  [micro_batch(): ffn_rows = lax.all_gather(ffn_in, 'ffn', axis=0, tiled=True)]
    ppermute x0 -> x6, waiting for transfers between devices: none -> 49.4 us  [micro_batch(): held = lax.ppermute(held, 'ffn', [(i, (i + 1) % size) for i in range(size)])]
    all_gather x2 -> x0, waiting for transfers between devices: 41.5 us -> none  [micro_batch(): grad_all = lax.all_gather(grad_rows_in, 'ffn', axis=0, tiled=True)]
    while x348 -> x354, local copies, waits for them, and re-layouts: 60.1 us -> 83.9 us
    while x40 -> x38, waiting for transfers between devices: 104 us -> 101 us
  transfers between devices with their start and end apart: 32 -> 36, of which waited for: 15 -> 15; matrix products, arithmetic and copies ran while one was open for 28% -> 30% of each run, Pallas kernels for 0% -> 0%
where the time goes in v1:
time: 1480 us; the launch traced here: 1470 us
  waiting for transfers between devices  749 us (51%)
  matrix products  226 us (15%)
  local copies, waits for them, and re-layouts  225 us (15%)
  blocking collectives  155 us (10%)
  other arithmetic  82.9 us (6%)
  between operations  15.8 us (1%)
    psum x1, waiting for transfers between devices, on_device(): lax.psum((totals[13], totals[14], totals[0], totals[1], totals[7], totals...  400 us
    reduce_scatter x1, waiting for transfers between devices, on_device(): lax.psum_scatter(attn_grad, ('dp', 'ffn'), scatter_dimension=0, tiled=True)  104 us
    while x38, waiting for transfers between devices  101 us
    while x354, local copies, waits for them, and re-layouts  83.9 us
    dot_general x22, matrix products, contract_rows(): lax.dot_general(left, right, (((0,), (0,)), ((), ())), preferred_element_...  78.6 us
    all_gather x2, blocking collectives, micro_batch(): lax.all_gather(own_keys[1], 'ffn', axis=0, tiled=True)  68.6 us
    dot_general x22, matrix products, matmul(): return jnp.dot(left, right, preferred_element_type=jnp.float32)  56.1 us
    reduce_scatter x2, waiting for transfers between devices, micro_batch(): lax.psum_scatter(times_transposed(grad_pre, w_up).astype(jnp.bfloat16), '...  50.4 us
  transfers between devices with their start and end apart: 36, of which 15 were waited for; matrix products, arithmetic and copies ran while one was open for 30% of the time, Pallas kernels for 0%

profile of v1, /device:TPU:0, one launch (start us, length us, event | category | flops | bytes accessed | tf_op | source)
XLA Modules:
  0.0 1472.2 jit_solution(10151193946812937605)
XLA Ops:
  15.3 876.9 %while.48 = (s32[]{:T(128)}, f32[1024]{0:T(1024)}, f32[1024]{0:T(1024)}, f32[1024,1024]{1,0:T(8,128)}, f32[1024,1024]{1,0:T(8,128)}, /*index=5*/f32[1024,1024]{1...) while((s32[]{:T(128)}, f32[1024]{0:T(1024)}, ...), condition=%wide.region_36.37_spmd.clone.clone, body=%wide.region_0.36_spmd.clone.clone.sunk | while | flops 15250011136 | bytes 711862336 | solution.py:305
  32.7 34.9 %all_gather.64 = bf16[384,1024]{1,0:T(8,128)(2,1)} all-gather(bf16[96,1024]{1,0:T(8,128)(2,1)S(1)} %convolution_convert_fusion.23), channel_id=1, replica_groups=mesh['dp'=8,'ffn'=4] {'ffn'}, dimensions={0}, use_global_device_ids=true | all-gather | bytes 983040 | tf_op jit(solution)/shard_map/while/body/eval_jaxpr/all_gather | solution.py:113
  76.2 11.7 add.894
  95.6 22.9 %all_gather.67 = bf16[384,1024]{1,0:T(8,128)(2,1)} all-gather(bf16[96,1024]{1,0:T(8,128)(2,1)S(1)} %convolution_convert_fusion.26), channel_id=1, replica_groups=mesh['dp'=8,'ffn'=4] {'ffn'}, dimensions={0}, use_global_device_ids=true | all-gather | bytes 983040 | tf_op jit(solution)/shard_map/while/body/eval_jaxpr/all_gather | solution.py:116
  135.3 20.3 %all-gather.12.cloned.1.call-done = bf16[512,1024]{1,0:T(8,128)(2,1)} async-done(((bf16[128,1024]{1,0:T(8,128)(2,1)}), bf16[512,1024]{1,0:T(8,128)(2,1)}) %all-gather.12.cloned.1.call-update) | async-done | bytes 1048592 | tf_op jit(solution)/shard_map/while/body/eval_jaxpr/all_gather | solution.py:115
  164.4 8.6 collective-permute-done.1
  173.6 16.1 %collective-permute-done.2 = bf16[128,1024]{1,0:T(8,128)(2,1)} collective-permute-done((bf16[128,1024]{1,0:T(8,128)(2,1)}, bf16[128,1024]{1,0:T(8,128)(2,1)}, u32[]{:S(2)}, u32[]{:S(2)}) %collective-permute-start.2) | collective-permute-done | bytes 262176 | tf_op jit(solution)/shard_map/while/body/eval_jaxpr/ppermute | solution.py:157
  203.1 8.2 multiply_convert_fusion.5
  222.9 25.1 %reduce-scatter.42.cloned.1.call-done = bf16[128,1024]{1,0:T(8,128)(2,1)} async-done(((bf16[512,1024]{1,0:T(8,128)(2,1)}), bf16[128,1024]{1,0:T(8,128)(2,1)}) %reduce-scatter.42.cloned.1.call-update) | async-done | bytes 262160 | tf_op jit(solution)/shard_map/while/body/eval_jaxpr/reduce_scatter | solution.py:166
  326.1 11.9 reshape.423
  338.0 10.8 reduce_sum.510
  373.4 8.8 reduce-scatter.46.cloned.1.call-done
  388.5 21.8 %reduce-scatter.48.cloned.1.call-done = bf16[128,1024]{1,0:T(8,128)(2,1)} async-done(((bf16[512,1024]{1,0:T(8,128)(2,1)}), bf16[128,1024]{1,0:T(8,128)(2,1)}) %reduce-scatter.48.cloned.1.call-update) | async-done | bytes 262160 | tf_op jit(solution)/shard_map/while
  412.8 25.6 %reduce-scatter.50.cloned.1.call-done = bf16[128,1024]{1,0:T(8,128)(2,1)} async-done(((bf16[512,1024]{1,0:T(8,128)(2,1)}), bf16[128,1024]{1,0:T(8,128)(2,1)}) %reduce-scatter.50.cloned.1.call-update) | async-done | bytes 262160 | tf_op jit(solution)/shard_map/while
  468.1 33.8 %all_gather.64 = bf16[384,1024]{1,0:T(8,128)(2,1)} all-gather(bf16[96,1024]{1,0:T(8,128)(2,1)S(1)} %convolution_convert_fusion.23), channel_id=1, replica_groups=mesh['dp'=8,'ffn'=4] {'ffn'}, dimensions={0}, use_global_device_ids=true | all-gather | bytes 983040 | tf_op jit(solution)/shard_map/while/body/eval_jaxpr/all_gather | solution.py:113
  510.4 11.6 add.894
  529.8 23.2 %all_gather.67 = bf16[384,1024]{1,0:T(8,128)(2,1)} all-gather(bf16[96,1024]{1,0:T(8,128)(2,1)S(1)} %convolution_convert_fusion.26), channel_id=1, replica_groups=mesh['dp'=8,'ffn'=4] {'ffn'}, dimensions={0}, use_global_device_ids=true | all-gather | bytes 983040 | tf_op jit(solution)/shard_map/while/body/eval_jaxpr/all_gather | solution.py:116
  569.8 21.8 %all-gather.12.cloned.1.call-done = bf16[512,1024]{1,0:T(8,128)(2,1)} async-done(((bf16[128,1024]{1,0:T(8,128)(2,1)}), bf16[512,1024]{1,0:T(8,128)(2,1)}) %all-gather.12.cloned.1.call-update) | async-done | bytes 1048592 | tf_op jit(solution)/shard_map/while/body/eval_jaxpr/all_gather | solution.py:115
  600.4 8.6 collective-permute-done.1
  609.2 16.1 %collective-permute-done.2 = bf16[128,1024]{1,0:T(8,128)(2,1)} collective-permute-done((bf16[128,1024]{1,0:T(8,128)(2,1)}, bf16[128,1024]{1,0:T(8,128)(2,1)}, u32[]{:S(2)}, u32[]{:S(2)}) %collective-permute-start.2) | collective-permute-done | bytes 262176 | tf_op jit(solution)/shard_map/while/body/eval_jaxpr/ppermute | solution.py:157
  638.8 8.2 multiply_convert_fusion.5
  658.5 25.3 %reduce-scatter.42.cloned.1.call-done = bf16[128,1024]{1,0:T(8,128)(2,1)} async-done(((bf16[512,1024]{1,0:T(8,128)(2,1)}), bf16[128,1024]{1,0:T(8,128)(2,1)}) %reduce-scatter.42.cloned.1.call-update) | async-done | bytes 262160 | tf_op jit(solution)/shard_map/while/body/eval_jaxpr/reduce_scatter | solution.py:166
  737.1 11.2 select_add_fusion.36
  770.2 11.9 reshape.423
  782.1 11.0 reduce_sum.510
  827.4 18.6 %reduce-scatter.48.cloned.1.call-done = bf16[128,1024]{1,0:T(8,128)(2,1)} async-done(((bf16[512,1024]{1,0:T(8,128)(2,1)}), bf16[128,1024]{1,0:T(8,128)(2,1)}) %reduce-scatter.48.cloned.1.call-update) | async-done | bytes 262160 | tf_op jit(solution)/shard_map/while
  848.5 25.5 %reduce-scatter.50.cloned.1.call-done = bf16[128,1024]{1,0:T(8,128)(2,1)} async-done(((bf16[512,1024]{1,0:T(8,128)(2,1)}), bf16[128,1024]{1,0:T(8,128)(2,1)}) %reduce-scatter.50.cloned.1.call-update) | async-done | bytes 262160 | tf_op jit(solution)/shard_map/while
  894.2 12.8 pad_maximum_fusion.1
  907.9 40.6 %all-reduce = (f32[1024]{0:T(1024)}, f32[1024]{0:T(1024)}, f32[8,22]{1,0:T(8,128)}, f32[1024]{0:T(1024)}, f32[1024]{0:T(1024)}, /*index=5*/f32[4096]{0:T(1024)}, f32[1024]{0:T(1024)}, f32[1024]{0:T(1024)}) all-reduce(f32[1024]{0:T(1024)S(1)} %copy-done.72, f32[1024]{0:T(1024)S(1)} %copy-done.75, ...), channel_id=1, replica_groups=mesh['dp'=8,'ffn'=4] {'dp','ffn'}, use_global_device_ids=true, to_apply=%region_37.38 | all-reduce | flops 10416 | bytes 83328 | tf_op jit(solution)/shard_map/psum | solution.py:315
  948.5 400.2 %all-reduce.3.cloned.1.call-done = f32[3072,1024]{1,0:T(8,128)} async-done(((f32[3072,1024]{1,0:T(8,128)}), f32[3072,1024]{1,0:T(8,128)}) %all-reduce.3.cloned.1.call-update) | async-done | bytes 12582928 | tf_op jit(solution)/shard_map/psum | solution.py:315
  1348.7 104.0 %reduce-scatter.36.cloned.1.call-done = f32[128,1024]{1,0:T(8,128)} async-done(((f32[4096,1024]{1,0:T(8,128)}), f32[128,1024]{1,0:T(8,128)}) %reduce-scatter.36.cloned.1.call-update) | async-done | bytes 524304 | tf_op jit(solution)/shard_map/reduce_scatter | solution.py:307
  1452.7 12.1 copy.197
  (701 shorter events, 422.7 us)
Async XLA Ops:
  15.6 103.0 %all-gather.6.cloned.1.call-start = ((), (), s32[]{:S(2)}) async-start(), calls=%async_computation.15 | async-start | bytes 1310720 | tf_op jit(solution)/shard_map/while/body/eval_jaxpr/all_gather | solution.py:114
  17.2 101.3 %all-gather.8.cloned.1.call-start = ((), (), s32[]{:S(2)}) async-start(), calls=%async_computation.16 | async-start | bytes 1310720 | tf_op jit(solution)/shard_map/while/body/eval_jaxpr/all_gather | solution.py:112
  18.9 116.4 %all-gather.10.cloned.1.call-start = ((), (), s32[]{:S(2)}) async-start(), calls=%async_computation.17 | async-start | bytes 1310720 | tf_op jit(solution)/shard_map/while/body/eval_jaxpr/all_gather | solution.py:117
  21.8 133.8 %all-gather.12.cloned.1.call-start = ((), (), s32[]{:S(2)}) async-start(), calls=%async_computation.18 | async-start | bytes 1310720 | tf_op jit(solution)/shard_map/while/body/eval_jaxpr/all_gather | solution.py:115
  24.2 138.8 %collective-permute-start = (bf16[128,1024]{1,0:T(8,128)(2,1)}, bf16[128,1024]{1,0:T(8,128)(2,1)}, u32[]{:S(2)}, u32[]{:S(2)}) collective-permute-start(bf16[128,1024]{1,0:T(8,128)(2,1)} %get-tuple-element.1430), channel_id=1, source_target_pairs={{0,1},{1,2},{2,3},{3,0},{4,5},{5,6},{6,7},{7,4},{8,9},{9,10},{10,1... | collective-permute-start | bytes 786440 | tf_op jit(solution)/shard_map/while/body/eval_jaxpr/ppermute | solution.py:157
  30.1 173.0 %all-gather.14.cloned.1.call-start = ((), (), s32[]{:S(2)}) async-start(), calls=%async_computation.19 | async-start | bytes 1310720 | tf_op jit(solution)/shard_map/while/body/eval_jaxpr/all_gather | solution.py:140
  162.9 85.1 %reduce-scatter.42.cloned.1.call-start = ((), (), s32[]{:S(2)}) async-start(), calls=%async_computation.20 | async-start | bytes 1310720 | tf_op jit(solution)/shard_map/while/body/eval_jaxpr/reduce_scatter | solution.py:166
  218.6 141.8 %reduce-scatter.56.cloned.1.call-start = ((), (), s32[]{:S(2)}) async-start(), calls=%async_computation.27 | async-start | bytes 1310720 | tf_op jit(solution)/shard_map/while/body/eval_jaxpr/reduce_scatter | solution.py:144
  222.9 139.4 %reduce-scatter.52.cloned.1.call-start = ((), (), s32[]{:S(2)}) async-start(), calls=%async_computation.25 | async-start | bytes 983040 | tf_op jit(solution)/shard_map/while
  270.0 96.8 %reduce-scatter.54.cloned.1.call-start = ((), (), s32[]{:S(2)}) async-start(), calls=%async_computation.26 | async-start | bytes 983040 | tf_op jit(solution)/shard_map/while
  279.0 92.7 %reduce-scatter.44.cloned.1.call-start = ((), (), s32[]{:S(2)}) async-start(), calls=%async_computation.21 | async-start | bytes 1310720 | tf_op jit(solution)/shard_map/while
  284.4 97.9 %reduce-scatter.46.cloned.1.call-start = ((), (), s32[]{:S(2)}) async-start(), calls=%async_computation.22 | async-start | bytes 1310720 | tf_op jit(solution)/shard_map/while
  289.9 120.4 %reduce-scatter.48.cloned.1.call-start = ((), (), s32[]{:S(2)}) async-start(), calls=%async_computation.23 | async-start | bytes 1310720 | tf_op jit(solution)/shard_map/while
  310.2 128.3 %reduce-scatter.50.cloned.1.call-start = ((), (), s32[]{:S(2)}) async-start(), calls=%async_computation.24 | async-start | bytes 1310720 | tf_op jit(solution)/shard_map/while
  453.9 99.1 %all-gather.6.cloned.1.call-start = ((), (), s32[]{:S(2)}) async-start(), calls=%async_computation.15 | async-start | bytes 1310720 | tf_op jit(solution)/shard_map/while/body/eval_jaxpr/all_gather | solution.py:114
  455.6 97.4 %all-gather.8.cloned.1.call-start = ((), (), s32[]{:S(2)}) async-start(), calls=%async_computation.16 | async-start | bytes 1310720 | tf_op jit(solution)/shard_map/while/body/eval_jaxpr/all_gather | solution.py:112
  457.3 112.5 %all-gather.10.cloned.1.call-start = ((), (), s32[]{:S(2)}) async-start(), calls=%async_computation.17 | async-start | bytes 1310720 | tf_op jit(solution)/shard_map/while/body/eval_jaxpr/all_gather | solution.py:117
  460.2 131.4 %all-gather.12.cloned.1.call-start = ((), (), s32[]{:S(2)}) async-start(), calls=%async_computation.18 | async-start | bytes 1310720 | tf_op jit(solution)/shard_map/while/body/eval_jaxpr/all_gather | solution.py:115
  462.6 136.4 %collective-permute-start = (bf16[128,1024]{1,0:T(8,128)(2,1)}, bf16[128,1024]{1,0:T(8,128)(2,1)}, u32[]{:S(2)}, u32[]{:S(2)}) collective-permute-start(bf16[128,1024]{1,0:T(8,128)(2,1)} %get-tuple-element.1430), channel_id=1, source_target_pairs={{0,1},{1,2},{2,3},{3,0},{4,5},{5,6},{6,7},{7,4},{8,9},{9,10},{10,1... | collective-permute-start | bytes 786440 | tf_op jit(solution)/shard_map/while/body/eval_jaxpr/ppermute | solution.py:157
  465.5 173.3 %all-gather.14.cloned.1.call-start = ((), (), s32[]{:S(2)}) async-start(), calls=%async_computation.19 | async-start | bytes 1310720 | tf_op jit(solution)/shard_map/while/body/eval_jaxpr/all_gather | solution.py:140
  598.9 84.9 %reduce-scatter.42.cloned.1.call-start = ((), (), s32[]{:S(2)}) async-start(), calls=%async_computation.20 | async-start | bytes 1310720 | tf_op jit(solution)/shard_map/while/body/eval_jaxpr/reduce_scatter | solution.py:166
  654.2 153.9 %reduce-scatter.56.cloned.1.call-start = ((), (), s32[]{:S(2)}) async-start(), calls=%async_computation.27 | async-start | bytes 1310720 | tf_op jit(solution)/shard_map/while/body/eval_jaxpr/reduce_scatter | solution.py:144
  658.5 151.4 %reduce-scatter.52.cloned.1.call-start = ((), (), s32[]{:S(2)}) async-start(), calls=%async_computation.25 | async-start | bytes 983040 | tf_op jit(solution)/shard_map/while
  705.8 108.7 %reduce-scatter.54.cloned.1.call-start = ((), (), s32[]{:S(2)}) async-start(), calls=%async_computation.26 | async-start | bytes 983040 | tf_op jit(solution)/shard_map/while
  714.8 104.5 %reduce-scatter.44.cloned.1.call-start = ((), (), s32[]{:S(2)}) async-start(), calls=%async_computation.21 | async-start | bytes 1310720 | tf_op jit(solution)/shard_map/while
  720.3 100.8 %reduce-scatter.46.cloned.1.call-start = ((), (), s32[]{:S(2)}) async-start(), calls=%async_computation.22 | async-start | bytes 1310720 | tf_op jit(solution)/shard_map/while
  725.8 120.2 %reduce-scatter.48.cloned.1.call-start = ((), (), s32[]{:S(2)}) async-start(), calls=%async_computation.23 | async-start | bytes 1310720 | tf_op jit(solution)/shard_map/while
  750.6 123.4 %reduce-scatter.50.cloned.1.call-start = ((), (), s32[]{:S(2)}) async-start(), calls=%async_computation.24 | async-start | bytes 1310720 | tf_op jit(solution)/shard_map/while
  892.2 456.5 %all-reduce.3.cloned.1.call-start = ((), (), s32[]{:S(2)}) async-start(), calls=%async_computation.14 | async-start | bytes 25165824 | tf_op jit(solution)/shard_map/psum | solution.py:315
  892.8 455.9 %reduce-scatter.38.cloned.1.call-start = ((), (), s32[]{:S(2)}) async-start(), calls=%async_computation.12 | async-start | bytes 4718592 | tf_op jit(solution)/shard_map/reduce_scatter | solution.py:309
  893.4 455.3 %reduce-scatter.40.cloned.1.call-start = ((), (), s32[]{:S(2)}) async-start(), calls=%async_computation.13 | async-start | bytes 4718592 | tf_op jit(solution)/shard_map/reduce_scatter | solution.py:310
  894.1 558.6 %reduce-scatter.36.cloned.1.call-start = ((), (), s32[]{:S(2)}) async-start(), calls=%async_computation.11 | async-start | bytes 17301504 | tf_op jit(solution)/shard_map/reduce_scatter | solution.py:307
  (185 other events, 1598.8 us)
Sparse Core Ops, SparseCore 0:
  18.5 46.1 all-gather.5
  66.3 26.1 all-gather.7
  94.2 32.3 all-gather.9
  128.0 27.5 all-gather.11
  163.0 33.0 all-gather.13
  218.7 29.2 reduce-scatter.41
  250.4 25.8 reduce-scatter.55
  278.6 21.9 reduce-scatter.51
  302.9 22.5 reduce-scatter.53
  327.6 26.4 reduce-scatter.43
  356.4 25.7 reduce-scatter.45
  384.4 25.7 reduce-scatter.47
  412.6 25.7 reduce-scatter.49
  456.6 44.3 all-gather.5
  502.4 26.1 all-gather.7
  530.0 32.2 all-gather.9
  563.8 27.7 all-gather.11
  599.0 33.0 all-gather.13
  654.4 29.3 reduce-scatter.41
  686.1 25.7 reduce-scatter.55
  714.2 21.9 reduce-scatter.51
  738.5 22.5 reduce-scatter.53
  763.4 26.3 reduce-scatter.43
  792.0 25.8 reduce-scatter.45
  820.2 25.7 reduce-scatter.47
  848.2 25.7 reduce-scatter.49
  897.2 51.9 reduce-scatter.37
  953.5 52.2 reduce-scatter.39
  1008.7 443.9 reduce-scatter.35
Sparse Core Ops, SparseCore 1:
  899.3 449.3 all-reduce.2
